TPU v7x, 512 devices: a whole 4x4x16 slice. The times are simulated.
512 devices in a mesh: doc: 16 (over y_hi, x, core), seq: 32 (over z, y_lo).
Axes of the slice: x: 4, y: 4 (y_hi: 2, y_lo: 2; y = y_hi * 2 + y_lo), z: 16, core: 2. Of those that a mesh axis runs over, the one named last changes fastest.
Arguments:
- queries: bfloat16 [16, 4096, 1024], P('doc', 'seq'), may hold values from -7 to 7
- key_rows: bfloat16 [16, 4096, 1024], P('doc', 'seq'), may hold values from -7 to 7
- value_rows: bfloat16 [16, 4096, 1024], P('doc', 'seq'), may hold values from -5 to 5
- cotangent: bfloat16 [16, 4096, 1024], P('doc', 'seq'), may hold values from -3 to 3
- out_weight: bfloat16 [1024, 1024], P('doc'), may hold values from -0.1875 to 0.1875
- lengths: int32 [16, 4], P('doc'), may hold values from 1 to 32, 64 in all within a row
- upweight: int32 [16, 4], P('doc'), may hold values from 1 to 6, as said below
Outputs:
- layer_out: bfloat16 [16, 4096, 1024], P('doc', 'seq')
- grad_query: bfloat16 [16, 4096, 1024], P('doc', 'seq')
- grad_key: bfloat16 [16, 4096, 1024], P('doc', 'seq')
- grad_value: bfloat16 [16, 4096, 1024], P('doc', 'seq')
- grad_weight: float32 [1024, 1024], P('doc')
Inputs may be any that keep to these rules, and one draw needn't show every extreme that they name: Each sequence's documents fill it exactly: the lengths add up to 64, and the longest is 32. `upweight`: each entry is 1 or 6; every sequence has a document with factor 6.
All inputs are finite; a program needn't handle non-finite values.
Results may differ from a plain program's by a relative error of at most 0.0089.
Values may be sent and summed in bfloat16 or wider, within the bound.
A program may use at most 128 MiB of HBM per device.

v0:
```python
import math
import jax
import jax.numpy as jnp
from jax import lax
from jax.sharding import PartitionSpec as P

HEADS = 16
HEAD_DIM = 64
WINDOW = 512
BLOCK = 64
DOCS = 4


def shifted(value, axis, steps):
    count = lax.axis_size(axis)
    first, last = (max(0, -steps), min(count, count - steps))
    return lax.ppermute(value, axis, [(source, source + steps) for source in range(first, last)])


def document_ids(lengths_row, positions):
    bounds = jnp.cumsum(lengths_row) * BLOCK
    return jnp.sum((positions[:, None] >= bounds[None, :]).astype(jnp.int32), axis=1)


def band_mask(query_pos, key_pos, query_doc, key_doc, seq_len):
    near_band = jnp.abs(query_pos[:, None] - key_pos[None, :]) <= WINDOW
    inside = (key_pos >= 0) & (key_pos < seq_len)
    return near_band & inside[None, :] & (query_doc[:, None] == key_doc[None, :])


def soft_weights(query_grp, key_grp, allowed):
    scores = jnp.einsum(
        "qhd,khd->hqk", query_grp, key_grp, preferred_element_type=jnp.float32
    ) * HEAD_DIM ** (-0.5)
    scores = jnp.where(allowed[None], scores, -jnp.inf)
    row_peak = jnp.max(scores, axis=2, keepdims=True)
    exponent = jnp.exp(scores - row_peak)
    return exponent / jnp.sum(exponent, axis=2, keepdims=True)


def body(queries, key_rows, value_rows, cotangent, out_weight, lengths, upweight):
    rows_here = queries.shape[1]
    model_width = queries.shape[2]
    seq_count = lax.axis_size("seq")
    doc_count = lax.axis_size("doc")
    seq_place = lax.axis_index("seq")
    seq_len = rows_here * seq_count
    edge_rows = min(WINDOW, rows_here)
    far_blocks = WINDOW // edge_rows
    key_span = rows_here + 2 * WINDOW
    score_scale = HEAD_DIM ** (-0.5)
    query_rows = queries[0]
    stacked = jnp.stack([key_rows[0], value_rows[0]])
    before_list = [shifted(stacked, "seq", distance) for distance in range(1, far_blocks + 1)]
    after_list = [shifted(stacked, "seq", -distance) for distance in range(1, far_blocks + 1)]
    extended = jnp.concatenate(before_list[::-1] + [stacked] + after_list, axis=1)
    key_ext = extended[0]
    value_ext = extended[1]
    row_base = seq_place * rows_here
    query_pos = row_base + jnp.arange(rows_here, dtype=jnp.int32)
    key_pos = row_base - WINDOW + jnp.arange(key_span, dtype=jnp.int32)
    lengths_row = lengths[0]
    query_doc = document_ids(lengths_row, query_pos)
    allowed = band_mask(query_pos, key_pos, query_doc, document_ids(lengths_row, key_pos), seq_len)
    matches = query_doc[:, None] == jnp.arange(DOCS, dtype=jnp.int32)[None, :]
    token_weight = jnp.sum(jnp.where(matches, upweight[0][None, :], 0), axis=1).astype(jnp.float32)
    group_heads = min(HEADS, max(1, 512 // rows_here))
    group_count = HEADS // group_heads
    group_cols = group_heads * HEAD_DIM

    def group_slices(group_index):
        col_start = group_index * group_cols
        query_grp = lax.dynamic_slice_in_dim(query_rows, col_start, group_cols, 1).reshape(
            rows_here, group_heads, HEAD_DIM
        )
        key_grp = lax.dynamic_slice_in_dim(key_ext, col_start, group_cols, 1).reshape(
            key_span, group_heads, HEAD_DIM
        )
        value_grp = lax.dynamic_slice_in_dim(value_ext, col_start, group_cols, 1).reshape(
            key_span, group_heads, HEAD_DIM
        )
        return (col_start, query_grp, key_grp, value_grp)

    def forward_group(group_index, attended_buf):
        col_start, query_grp, key_grp, value_grp = group_slices(group_index)
        prob_half = soft_weights(query_grp, key_grp, allowed).astype(jnp.bfloat16)
        mixed_rows = jnp.einsum(
            "hqk,khd->qhd", prob_half, value_grp, preferred_element_type=jnp.float32
        )
        mixed_rows = mixed_rows.reshape(rows_here, group_cols).astype(jnp.bfloat16)
        return lax.dynamic_update_slice_in_dim(attended_buf, mixed_rows, col_start, 1)

    attended = lax.fori_loop(
        0, group_count, forward_group, jnp.zeros((rows_here, model_width), jnp.bfloat16)
    )
    full_weight = lax.all_gather(out_weight, "doc", axis=0, tiled=True)
    layer_out = jnp.dot(attended, full_weight, preferred_element_type=jnp.float32).astype(
        jnp.bfloat16
    )
    grad_out = (token_weight[:, None] * cotangent[0].astype(jnp.float32)).astype(jnp.bfloat16)
    grad_attended = lax.dot_general(
        grad_out, full_weight, (((1,), (1,)), ((), ())), preferred_element_type=jnp.float32
    ).astype(jnp.bfloat16)
    partial_grad = lax.dot_general(
        attended, grad_out, (((0,), (0,)), ((), ())), preferred_element_type=jnp.float32
    )
    row_block = lax.psum_scatter(partial_grad, "doc", scatter_dimension=0, tiled=True)
    weight_sum = lax.psum(row_block, "seq")
    grad_weight = weight_sum * (1.0 / math.sqrt(rows_here * seq_count * doc_count))

    def backward_group(group_index, grad_state):
        grad_query_buf, own_grad, early_grad, later_grad = grad_state
        col_start, query_grp, key_grp, value_grp = group_slices(group_index)
        prob_full = soft_weights(query_grp, key_grp, allowed)
        prob_half = prob_full.astype(jnp.bfloat16)
        grad_grp = lax.dynamic_slice_in_dim(grad_attended, col_start, group_cols, 1).reshape(
            rows_here, group_heads, HEAD_DIM
        )
        grad_prob = jnp.einsum(
            "qhd,khd->hqk", grad_grp, value_grp, preferred_element_type=jnp.float32
        )
        centre = jnp.sum(prob_full * grad_prob, axis=2, keepdims=True)
        grad_score = (prob_full * (grad_prob - centre) * score_scale).astype(jnp.bfloat16)
        grad_query_grp = jnp.einsum(
            "hqk,khd->qhd", grad_score, key_grp, preferred_element_type=jnp.float32
        )
        grad_query_grp = grad_query_grp.reshape(rows_here, group_cols).astype(jnp.bfloat16)
        key_part = jnp.einsum(
            "hqk,qhd->khd", grad_score, query_grp, preferred_element_type=jnp.float32
        )
        value_part = jnp.einsum(
            "hqk,qhd->khd", prob_half, grad_grp, preferred_element_type=jnp.float32
        )
        both_parts = jnp.stack(
            [key_part.reshape(key_span, group_cols), value_part.reshape(key_span, group_cols)]
        )
        grad_query_buf = lax.dynamic_update_slice_in_dim(
            grad_query_buf, grad_query_grp, col_start, 1
        )
        own_grad = lax.dynamic_update_slice(
            own_grad, both_parts[:, WINDOW : WINDOW + rows_here], (0, 0, col_start)
        )
        early_grad = lax.dynamic_update_slice(
            early_grad, both_parts[:, :WINDOW].astype(jnp.bfloat16), (0, 0, col_start)
        )
        later_grad = lax.dynamic_update_slice(
            later_grad, both_parts[:, WINDOW + rows_here :].astype(jnp.bfloat16), (0, 0, col_start)
        )
        return (grad_query_buf, own_grad, early_grad, later_grad)

    grad_state = (
        jnp.zeros((rows_here, model_width), jnp.bfloat16),
        jnp.zeros((2, rows_here, model_width), jnp.float32),
        jnp.zeros((2, WINDOW, model_width), jnp.bfloat16),
        jnp.zeros((2, WINDOW, model_width), jnp.bfloat16),
    )
    grad_query, own_grad, early_grad, later_grad = lax.fori_loop(
        0, group_count, backward_group, grad_state
    )
    early_returned = [
        shifted(
            early_grad[:, WINDOW - distance * edge_rows : WINDOW - (distance - 1) * edge_rows],
            "seq",
            -distance,
        )
        for distance in range(1, far_blocks + 1)
    ]
    later_returned = [
        shifted(later_grad[:, (distance - 1) * edge_rows : distance * edge_rows], "seq", distance)
        for distance in range(1, far_blocks + 1)
    ]
    tail_extra = jnp.zeros((2, edge_rows, model_width), jnp.float32)
    for returned in early_returned:
        tail_extra = tail_extra + returned.astype(jnp.float32)
    head_extra = jnp.zeros((2, edge_rows, model_width), jnp.float32)
    for returned in later_returned:
        head_extra = head_extra + returned.astype(jnp.float32)
    own_grad = own_grad.at[:, rows_here - edge_rows :].add(tail_extra)
    own_grad = own_grad.at[:, :edge_rows].add(head_extra)
    grad_key = own_grad[0].astype(jnp.bfloat16)
    grad_value = own_grad[1].astype(jnp.bfloat16)
    return (layer_out[None], grad_query[None], grad_key[None], grad_value[None], grad_weight)


def solution(mesh):
    return jax.shard_map(
        body,
        mesh=mesh,
        in_specs=(
            P("doc", "seq", None),
            P("doc", "seq", None),
            P("doc", "seq", None),
            P("doc", "seq", None),
            P("doc", None),
            P("doc", None),
            P("doc", None),
        ),
        out_specs=(
            P("doc", "seq", None),
            P("doc", "seq", None),
            P("doc", "seq", None),
            P("doc", "seq", None),
            P("doc", None),
        ),
        check_vma=False,
    )
```

profile of v0, /device:TPU:2, one launch (start us, length us, event | category | flops | bytes accessed | tf_op | source)
XLA Modules:
  0.0 587.8 jit_solution(5047850334984720192)
XLA Ops:
  9.6 6.0 %collective-permute-start = (bf16[2,128,1024]{1,2,0:T(8,128)(2,1)S(1)}, bf16[2,128,1024]{1,2,0:T(8,128)(2,1)}, u32[]{:S(2)}, u32[]{:S(2)}) collective-permute-start(bf16[2,128,1024]{1,2,0:T(8,128)(2,1)S(1)} %pad_maximum_fusion.1), channel_id=1, source_target_pairs={{0,4},{1,5},{2,6},{3,7},{4,8},{5,9},{6,10},{7,11},{8,12},{9,13},{1... | collective-permute-start | bytes 1572872 | tf_op jit(solution)/shard_map/ppermute | solution.py:17
  15.5 4.9 collective-permute-start.1
  20.4 4.3 collective-permute-start.2
  24.7 3.7 collective-permute-start.3
  28.4 1.3 collective-permute-start.4
  32.4 1.3 collective-permute-start.5
  34.9 6.6 %collective-permute-done.1 = bf16[2,128,1024]{1,2,0:T(8,128)(2,1)S(1)} collective-permute-done((bf16[2,128,1024]{1,2,0:T(8,128)(2,1)S(1)}, bf16[2,128,1024]{1,2,0:T(8,128)(2,1)S(1)}, u32[]{:S(2)}, u32[]{:S(2)}) %collective-permute-start.1) | collective-permute-done | bytes 524320 | tf_op jit(solution)/shard_map/ppermute | solution.py:17
  41.5 1.3 collective-permute-start.6
  42.9 8.7 %collective-permute-done.2 = bf16[2,128,1024]{1,2,0:T(8,128)(2,1)S(1)} collective-permute-done((bf16[2,128,1024]{1,2,0:T(8,128)(2,1)S(1)}, bf16[2,128,1024]{1,2,0:T(8,128)(2,1)S(1)}, u32[]{:S(2)}, u32[]{:S(2)}) %collective-permute-start.2) | collective-permute-done | bytes 524320 | tf_op jit(solution)/shard_map/ppermute | solution.py:17
  51.6 1.3 collective-permute-start.7
  53.4 1.7 collective-permute-done.5
  55.2 21.0 %collective-permute-done.6 = bf16[2,128,1024]{1,2,0:T(8,128)(2,1)S(1)} collective-permute-done((bf16[2,128,1024]{1,2,0:T(8,128)(2,1)S(1)}, bf16[2,128,1024]{1,2,0:T(8,128)(2,1)S(1)}, u32[]{:S(2)}, u32[]{:S(2)}) %collective-permute-start.6) | collective-permute-done | bytes 524320 | tf_op jit(solution)/shard_map/ppermute | solution.py:17
  76.3 30.6 %collective-permute-done.7 = bf16[2,128,1024]{1,2,0:T(8,128)(2,1)S(1)} collective-permute-done((bf16[2,128,1024]{1,2,0:T(8,128)(2,1)S(1)}, bf16[2,128,1024]{1,2,0:T(8,128)(2,1)S(1)}, u32[]{:S(2)}, u32[]{:S(2)}) %collective-permute-start.7) | collective-permute-done | bytes 524320 | tf_op jit(solution)/shard_map/ppermute | solution.py:17
  107.0 2.5 slice_bitcast_fusion
  109.6 29.0 %while.38 = (s32[]{:T(128)}, bf16[128,1024]{0,1:T(8,128)(2,1)S(1)}, bf16[1152,1024]{0,1:T(8,128)(2,1)}, bf16[128,1024]{0,1:T(8,128)(2,1)}, bf16[1152,1024]{0,1:T...) while((s32[]{:T(128)}, bf16[128,1024]{0,1:T(8,128)(2,1)S(1)}, ...), condition=%wide.region_6.7_spmd.clone, body=%wide.region_3.6_spmd.clone.sunk | while | flops 155452544 | bytes 8961351 | solution.py:93
  109.7 1.4 constant_dynamic-slice_fusion.13
  112.2 2.4 fusion.104
  114.6 2.3 fusion.105
  116.9 1.3 constant_dynamic-slice_fusion.13
  119.4 2.4 fusion.104
  121.8 2.3 fusion.105
  124.2 1.3 constant_dynamic-slice_fusion.13
  126.7 2.4 fusion.104
  129.0 2.3 fusion.105
  131.4 1.3 constant_dynamic-slice_fusion.13
  133.9 2.4 fusion.104
  136.3 2.3 fusion.105
  138.6 2.7 fusion.51
  141.7 3.1 convolution_convert_fusion
  146.7 1.6 broadcast.133.clone
  148.2 1.6 broadcast.133.clone2
  149.8 94.7 %while.39 = (s32[]{:T(128)}, bf16[128,1024]{1,0:T(8,128)(2,1)}, f32[2,128,1024]{2,1,0:T(8,128)}, bf16[2,512,1024]{2,1,0:T(8,128)(2,1)}, bf16[2,512,1024]{2,1,0:T...) while((s32[]{:T(128)}, bf16[128,1024]{1,0:T(8,128)(2,1)}, ...), condition=%wide.region_12.13_spmd.clone, body=%wide.region_8.12_spmd.clone.sunk | while | flops 390861184 | bytes 38351472 | solution.py:157
  155.4 2.4 fusion.118
  157.8 4.7 fusion.119
  163.4 5.2 fusion.120
  168.6 2.2 fusion.121
  179.4 2.4 fusion.118
  181.8 4.7 fusion.119
  187.3 5.0 fusion.120
  192.4 2.1 fusion.121
  203.0 2.4 fusion.118
  205.4 4.7 fusion.119
  210.9 5.0 fusion.120
  216.0 2.1 fusion.121
  226.5 2.4 fusion.118
  228.9 4.7 fusion.119
  234.4 5.2 fusion.120
  239.6 2.1 fusion.121
  244.6 2.7 fusion.58
  247.3 11.6 %collective-permute-start.15 = (bf16[2,128,1024]{2,1,0:T(8,128)(2,1)S(1)}, bf16[2,128,1024]{2,1,0:T(8,128)(2,1)S(1)}, u32[]{:S(2)}, u32[]{:S(2)}) collective-permute-start(bf16[2,128,1024]{2,1,0:T(8,128)(2,1)S(1)} %get-tuple-element.488), channel_id=1, source_target_pairs={{0,4},{1,5},{2,6},{3,7},{4,8},{5,9},{6,10},{7,11},{8,12},{9,13},{1... | collective-permute-start | bytes 1572872 | tf_op jit(solution)/shard_map/ppermute | solution.py:17
  258.8 1.3 collective-permute-start.14
  260.2 1.3 collective-permute-start.13
  261.5 6.2 %collective-permute-start.12 = (bf16[2,128,1024]{2,1,0:T(8,128)(2,1)}, bf16[2,128,1024]{2,1,0:T(8,128)(2,1)S(1)}, u32[]{:S(2)}, u32[]{:S(2)}) collective-permute-start(bf16[2,128,1024]{2,1,0:T(8,128)(2,1)} %get-tuple-element.485), channel_id=1, source_target_pairs={{0,1},{1,2},{2,3},{3,4},{4,5},{5,6},{6,7},{7,8},{8,9},{9,10},{10,1... | collective-permute-start | bytes 1572872 | tf_op jit(solution)/shard_map/ppermute | solution.py:17
  267.7 1.3 fusion.57
  269.0 1.4 collective-permute-start.11
  271.1 1.3 collective-permute-start.10
  272.4 10.0 %collective-permute-done.14 = bf16[2,128,1024]{2,1,0:T(8,128)(2,1)S(1)} collective-permute-done((bf16[2,128,1024]{2,1,0:T(8,128)(2,1)S(1)}, bf16[2,128,1024]{2,1,0:T(8,128)(2,1)S(1)}, u32[]{:S(2)}, u32[]{:S(2)}) %collective-permute-start.14) | collective-permute-done | bytes 524320 | tf_op jit(solution)/shard_map/ppermute | solution.py:17
  282.4 1.3 collective-permute-start.9
  283.7 8.7 %collective-permute-done.13 = bf16[2,128,1024]{2,1,0:T(8,128)(2,1)S(1)} collective-permute-done((bf16[2,128,1024]{2,1,0:T(8,128)(2,1)S(1)}, bf16[2,128,1024]{2,1,0:T(8,128)(2,1)S(1)}, u32[]{:S(2)}, u32[]{:S(2)}) %collective-permute-start.13) | collective-permute-done | bytes 524320 | tf_op jit(solution)/shard_map/ppermute | solution.py:17
  294.9 6.7 %collective-permute-done.10 = bf16[2,128,1024]{2,1,0:T(8,128)(2,1)} collective-permute-done((bf16[2,128,1024]{2,1,0:T(8,128)(2,1)}, bf16[2,128,1024]{2,1,0:T(8,128)(2,1)}, u32[]{:S(2)}, u32[]{:S(2)}) %collective-permute-start.10) | collective-permute-done | bytes 524320 | tf_op jit(solution)/shard_map/ppermute | solution.py:17
  301.6 10.5 %collective-permute-done.9 = bf16[2,128,1024]{2,1,0:T(8,128)(2,1)} collective-permute-done((bf16[2,128,1024]{2,1,0:T(8,128)(2,1)}, bf16[2,128,1024]{2,1,0:T(8,128)(2,1)}, u32[]{:S(2)}, u32[]{:S(2)}) %collective-permute-start.9) | collective-permute-done | bytes 524320 | tf_op jit(solution)/shard_map/ppermute | solution.py:17
  312.6 2.4 add_convert_fusion
  315.9 263.7 %all-reduce.2.cloned.1.call-done = f32[64,1024]{1,0:T(8,128)} async-done(((f32[64,1024]{1,0:T(8,128)}), f32[64,1024]{1,0:T(8,128)}) %all-reduce.2.cloned.1.call-update) | async-done | bytes 262160 | tf_op jit(solution)/shard_map/psum | solution.py:108
  579.6 1.7 broadcast_multiply_fusion
  (209 shorter events, 55.0 us)
Async XLA Ops:
  7.2 24.3 %copy-start.8 = (bf16[1,128,1024]{2,1,0:T(8,128)(2,1)S(1)}, bf16[1,128,1024]{2,1,0:T(8,128)(2,1)}, u32[]{:S(2)}) copy-start(bf16[1,128,1024]{2,1,0:T(8,128)(2,1)} %param.19) | copy-start | bytes 786436
  7.2 134.5 %all-gather.2.cloned.1.call-start = ((), (), s32[]{:S(2)}) async-start(), calls=%async_computation.1 | async-start | bytes 2228224 | tf_op jit(solution)/shard_map/all_gather | solution.py:96
  9.6 22.9 %collective-permute-start = (bf16[2,128,1024]{1,2,0:T(8,128)(2,1)S(1)}, bf16[2,128,1024]{1,2,0:T(8,128)(2,1)}, u32[]{:S(2)}, u32[]{:S(2)}) collective-permute-start(bf16[2,128,1024]{1,2,0:T(8,128)(2,1)S(1)} %pad_maximum_fusion.1), channel_id=1, source_target_pairs={{0,4},{1,5},{2,6},{3,7},{4,8},{5,9},{6,10},{7,11},{8,12},{9,13},{1... | collective-permute-start | bytes 1572872 | tf_op jit(solution)/shard_map/ppermute | solution.py:17
  15.5 26.0 %collective-permute-start.1 = (bf16[2,128,1024]{1,2,0:T(8,128)(2,1)S(1)}, bf16[2,128,1024]{1,2,0:T(8,128)(2,1)S(1)}, u32[]{:S(2)}, u32[]{:S(2)}) collective-permute-start(bf16[2,128,1024]{1,2,0:T(8,128)(2,1)S(1)} %pad_maximum_fusion.1), channel_id=1, source_target_pairs={{0,3},{1,4},{2,5},{3,6},{4,7},{5,8},{6,9},{7,10},{8,11},{9,12},{10... | collective-permute-start | bytes 1572872 | tf_op jit(solution)/shard_map/ppermute | solution.py:17
  20.4 31.2 %collective-permute-start.2 = (bf16[2,128,1024]{1,2,0:T(8,128)(2,1)S(1)}, bf16[2,128,1024]{1,2,0:T(8,128)(2,1)S(1)}, u32[]{:S(2)}, u32[]{:S(2)}) collective-permute-start(bf16[2,128,1024]{1,2,0:T(8,128)(2,1)S(1)} %pad_maximum_fusion.1), channel_id=1, source_target_pairs={{0,2},{1,3},{2,4},{3,5},{4,6},{5,7},{6,8},{7,9},{8,10},{9,11},{10,... | collective-permute-start | bytes 1572872 | tf_op jit(solution)/shard_map/ppermute | solution.py:17
  24.7 28.3 %collective-permute-start.3 = (bf16[2,128,1024]{1,2,0:T(8,128)(2,1)S(1)}, bf16[2,128,1024]{1,2,0:T(8,128)(2,1)S(1)}, u32[]{:S(2)}, u32[]{:S(2)}) collective-permute-start(bf16[2,128,1024]{1,2,0:T(8,128)(2,1)S(1)} %pad_maximum_fusion.1), channel_id=1, source_target_pairs={{0,1},{1,2},{2,3},{3,4},{4,5},{5,6},{6,7},{7,8},{8,9},{9,10},{10,1... | collective-permute-start | bytes 1572872 | tf_op jit(solution)/shard_map/ppermute | solution.py:17
  28.4 24.9 %collective-permute-start.4 = (bf16[2,128,1024]{1,2,0:T(8,128)(2,1)S(1)}, bf16[2,128,1024]{1,2,0:T(8,128)(2,1)S(1)}, u32[]{:S(2)}, u32[]{:S(2)}) collective-permute-start(bf16[2,128,1024]{1,2,0:T(8,128)(2,1)S(1)} %pad_maximum_fusion.1), channel_id=1, source_target_pairs={{1,0},{2,1},{3,2},{4,3},{5,4},{6,5},{7,6},{8,7},{9,8},{10,9},{11,1... | collective-permute-start | bytes 1572872 | tf_op jit(solution)/shard_map/ppermute | solution.py:17
  29.7 265.1 %reduce-scatter.2.cloned.1.call-start = ((), (), s32[]{:S(2)}) async-start(), calls=%async_computation.2 | async-start | bytes 4456448 | tf_op jit(solution)/shard_map/reduce_scatter | solution.py:107
  32.4 22.7 %collective-permute-start.5 = (bf16[2,128,1024]{1,2,0:T(8,128)(2,1)S(1)}, bf16[2,128,1024]{1,2,0:T(8,128)(2,1)S(1)}, u32[]{:S(2)}, u32[]{:S(2)}) collective-permute-start(bf16[2,128,1024]{1,2,0:T(8,128)(2,1)S(1)} %pad_maximum_fusion.1), channel_id=1, source_target_pairs={{2,0},{3,1},{4,2},{5,3},{6,4},{7,5},{8,6},{9,7},{10,8},{11,9},{12,... | collective-permute-start | bytes 1572872 | tf_op jit(solution)/shard_map/ppermute | solution.py:17
  41.5 34.7 %collective-permute-start.6 = (bf16[2,128,1024]{1,2,0:T(8,128)(2,1)S(1)}, bf16[2,128,1024]{1,2,0:T(8,128)(2,1)S(1)}, u32[]{:S(2)}, u32[]{:S(2)}) collective-permute-start(bf16[2,128,1024]{1,2,0:T(8,128)(2,1)S(1)} %pad_maximum_fusion.1), channel_id=1, source_target_pairs={{3,0},{4,1},{5,2},{6,3},{7,4},{8,5},{9,6},{10,7},{11,8},{12,9},{13... | collective-permute-start | bytes 1572872 | tf_op jit(solution)/shard_map/ppermute | solution.py:17
  51.6 55.3 %collective-permute-start.7 = (bf16[2,128,1024]{1,2,0:T(8,128)(2,1)S(1)}, bf16[2,128,1024]{1,2,0:T(8,128)(2,1)S(1)}, u32[]{:S(2)}, u32[]{:S(2)}) collective-permute-start(bf16[2,128,1024]{1,2,0:T(8,128)(2,1)S(1)} %pad_maximum_fusion.1), channel_id=1, source_target_pairs={{4,0},{5,1},{6,2},{7,3},{8,4},{9,5},{10,6},{11,7},{12,8},{13,9},{1... | collective-permute-start | bytes 1572872 | tf_op jit(solution)/shard_map/ppermute | solution.py:17
  109.6 29.0 %copy-start.7 = (bf16[1,128,1024]{2,1,0:T(8,128)(2,1)S(1)}, bf16[1,128,1024]{2,1,0:T(8,128)(2,1)}, u32[]{:S(2)}) copy-start(bf16[1,128,1024]{2,1,0:T(8,128)(2,1)} %param.22) | copy-start | bytes 786436
  138.6 2.8 copy-start.4
  141.4 438.2 %all-reduce.2.cloned.1.call-start = ((), (), s32[]{:S(2)}) async-start(), calls=%async_computation.3 | async-start | bytes 524288 | tf_op jit(solution)/shard_map/psum | solution.py:108
  149.8 3.2 copy-start.9
  149.8 3.3 copy-start.11
  149.8 3.3 copy-start.13
  151.9 10.7 %copy-start.2 = (bf16[128,256]{0,1:T(8,128)(2,1)}, bf16[128,256]{0,1:T(8,128)(2,1)S(1)}, u32[]{:S(2)}) copy-start(bf16[128,256]{0,1:T(8,128)(2,1)S(1)} %copy.54) | copy-start | bytes 196612 | tf_op jit(solution)/shard_map/while
  154.5 8.1 %copy-start.6 = (bf16[128,256]{0,1:T(8,128)(2,1)}, bf16[128,256]{0,1:T(8,128)(2,1)S(1)}, u32[]{:S(2)}) copy-start(bf16[128,256]{0,1:T(8,128)(2,1)S(1)} %constant_dynamic-slice_fusion.18) | copy-start | bytes 196612 | tf_op jit(solution)/shard_map/while
  157.8 4.8 copy-start.15
  172.1 1.6 copy-start.10
  172.1 1.6 copy-start.12
  172.1 1.6 copy-start.14
  173.7 3.4 copy-start.9
  173.7 3.4 copy-start.11
  173.7 3.4 copy-start.13
  175.9 10.7 %copy-start.2 = (bf16[128,256]{0,1:T(8,128)(2,1)}, bf16[128,256]{0,1:T(8,128)(2,1)S(1)}, u32[]{:S(2)}) copy-start(bf16[128,256]{0,1:T(8,128)(2,1)S(1)} %copy.54) | copy-start | bytes 196612 | tf_op jit(solution)/shard_map/while
  178.4 8.1 %copy-start.6 = (bf16[128,256]{0,1:T(8,128)(2,1)}, bf16[128,256]{0,1:T(8,128)(2,1)S(1)}, u32[]{:S(2)}) copy-start(bf16[128,256]{0,1:T(8,128)(2,1)S(1)} %constant_dynamic-slice_fusion.18) | copy-start | bytes 196612 | tf_op jit(solution)/shard_map/while
  181.8 4.8 copy-start.15
  195.7 1.5 copy-start.10
  195.7 1.5 copy-start.12
  195.7 1.5 copy-start.14
  197.3 3.3 copy-start.9
  197.3 3.3 copy-start.11
  197.3 3.3 copy-start.13
  199.4 10.7 %copy-start.2 = (bf16[128,256]{0,1:T(8,128)(2,1)}, bf16[128,256]{0,1:T(8,128)(2,1)S(1)}, u32[]{:S(2)}) copy-start(bf16[128,256]{0,1:T(8,128)(2,1)S(1)} %copy.54) | copy-start | bytes 196612 | tf_op jit(solution)/shard_map/while
  202.0 8.1 %copy-start.6 = (bf16[128,256]{0,1:T(8,128)(2,1)}, bf16[128,256]{0,1:T(8,128)(2,1)S(1)}, u32[]{:S(2)}) copy-start(bf16[128,256]{0,1:T(8,128)(2,1)S(1)} %constant_dynamic-slice_fusion.18) | copy-start | bytes 196612 | tf_op jit(solution)/shard_map/while
  205.4 4.8 copy-start.15
  219.3 1.5 copy-start.10
  219.3 1.5 copy-start.12
  219.3 1.5 copy-start.14
  220.8 3.3 copy-start.9
  220.9 3.3 copy-start.11
  220.9 3.3 copy-start.13
  223.0 10.7 %copy-start.2 = (bf16[128,256]{0,1:T(8,128)(2,1)}, bf16[128,256]{0,1:T(8,128)(2,1)S(1)}, u32[]{:S(2)}) copy-start(bf16[128,256]{0,1:T(8,128)(2,1)S(1)} %copy.54) | copy-start | bytes 196612 | tf_op jit(solution)/shard_map/while
  225.5 8.1 %copy-start.6 = (bf16[128,256]{0,1:T(8,128)(2,1)}, bf16[128,256]{0,1:T(8,128)(2,1)S(1)}, u32[]{:S(2)}) copy-start(bf16[128,256]{0,1:T(8,128)(2,1)S(1)} %constant_dynamic-slice_fusion.18) | copy-start | bytes 196612 | tf_op jit(solution)/shard_map/while
  228.9 4.8 copy-start.15
  243.0 1.6 copy-start.10
  243.0 1.6 copy-start.12
  243.0 1.6 copy-start.14
  244.6 23.1 %copy-start.1 = (bf16[2,512,1024]{2,1,0:T(8,128)(2,1)S(1)}, bf16[2,512,1024]{2,1,0:T(8,128)(2,1)}, u32[]{:S(2)}) copy-start(bf16[2,512,1024]{2,1,0:T(8,128)(2,1)} %get-tuple-element.329) | copy-start | bytes 6291460
  247.3 46.4 %copy-start = (bf16[1024,1024]{1,0:T(8,128)(2,1)S(1)}, bf16[1024,1024]{1,0:T(8,128)(2,1)}, u32[]{:S(2)}) copy-start(bf16[1024,1024]{1,0:T(8,128)(2,1)} %all-gather.2.cloned.1.call-done) | copy-start | bytes 6291460
  247.3 46.4 %copy-start.5 = (bf16[128,1024]{0,1:T(8,128)(2,1)S(1)}, bf16[128,1024]{0,1:T(8,128)(2,1)}, u32[]{:S(2)}) copy-start(bf16[128,1024]{0,1:T(8,128)(2,1)} %copy-done.4) | copy-start | bytes 786436
  247.3 23.9 %collective-permute-start.15 = (bf16[2,128,1024]{2,1,0:T(8,128)(2,1)S(1)}, bf16[2,128,1024]{2,1,0:T(8,128)(2,1)S(1)}, u32[]{:S(2)}, u32[]{:S(2)}) collective-permute-start(bf16[2,128,1024]{2,1,0:T(8,128)(2,1)S(1)} %get-tuple-element.488), channel_id=1, source_target_pairs={{0,4},{1,5},{2,6},{3,7},{4,8},{5,9},{6,10},{7,11},{8,12},{9,13},{1... | collective-permute-start | bytes 1572872 | tf_op jit(solution)/shard_map/ppermute | solution.py:17
  258.8 23.6 %collective-permute-start.14 = (bf16[2,128,1024]{2,1,0:T(8,128)(2,1)S(1)}, bf16[2,128,1024]{2,1,0:T(8,128)(2,1)S(1)}, u32[]{:S(2)}, u32[]{:S(2)}) collective-permute-start(bf16[2,128,1024]{2,1,0:T(8,128)(2,1)S(1)} %get-tuple-element.486), channel_id=1, source_target_pairs={{0,3},{1,4},{2,5},{3,6},{4,7},{5,8},{6,9},{7,10},{8,11},{9,12},{10... | collective-permute-start | bytes 1572872 | tf_op jit(solution)/shard_map/ppermute | solution.py:17
  260.2 32.2 %collective-permute-start.13 = (bf16[2,128,1024]{2,1,0:T(8,128)(2,1)S(1)}, bf16[2,128,1024]{2,1,0:T(8,128)(2,1)S(1)}, u32[]{:S(2)}, u32[]{:S(2)}) collective-permute-start(bf16[2,128,1024]{2,1,0:T(8,128)(2,1)S(1)} %get-tuple-element.487), channel_id=1, source_target_pairs={{0,2},{1,3},{2,4},{3,5},{4,6},{5,7},{6,8},{7,9},{8,10},{9,11},{10,... | collective-permute-start | bytes 1572872 | tf_op jit(solution)/shard_map/ppermute | solution.py:17
  261.5 33.4 %collective-permute-start.12 = (bf16[2,128,1024]{2,1,0:T(8,128)(2,1)}, bf16[2,128,1024]{2,1,0:T(8,128)(2,1)S(1)}, u32[]{:S(2)}, u32[]{:S(2)}) collective-permute-start(bf16[2,128,1024]{2,1,0:T(8,128)(2,1)} %get-tuple-element.485), channel_id=1, source_target_pairs={{0,1},{1,2},{2,3},{3,4},{4,5},{5,6},{6,7},{7,8},{8,9},{9,10},{10,1... | collective-permute-start | bytes 1572872 | tf_op jit(solution)/shard_map/ppermute | solution.py:17
  269.0 43.6 %copy-start.3 = (f32[2,128,1024]{2,1,0:T(8,128)S(1)}, f32[2,128,1024]{2,1,0:T(8,128)}, u32[]{:S(2)}) copy-start(f32[2,128,1024]{2,1,0:T(8,128)} %get-tuple-element.328) | copy-start | bytes 3145732
  269.0 25.9 %collective-permute-start.11 = (bf16[2,128,1024]{2,1,0:T(8,128)(2,1)}, bf16[2,128,1024]{2,1,0:T(8,128)(2,1)}, u32[]{:S(2)}, u32[]{:S(2)}) collective-permute-start(bf16[2,128,1024]{2,1,0:T(8,128)(2,1)} %get-tuple-element.484), channel_id=1, source_target_pairs={{4,0},{5,1},{6,2},{7,3},{8,4},{9,5},{10,6},{11,7},{12,8},{13,9},{1... | collective-permute-start | bytes 1572872 | tf_op jit(solution)/shard_map/ppermute | solution.py:17
  271.1 30.4 %collective-permute-start.10 = (bf16[2,128,1024]{2,1,0:T(8,128)(2,1)}, bf16[2,128,1024]{2,1,0:T(8,128)(2,1)}, u32[]{:S(2)}, u32[]{:S(2)}) collective-permute-start(bf16[2,128,1024]{2,1,0:T(8,128)(2,1)} %get-tuple-element.482), channel_id=1, source_target_pairs={{3,0},{4,1},{5,2},{6,3},{7,4},{8,5},{9,6},{10,7},{11,8},{12,9},{13... | collective-permute-start | bytes 1572872 | tf_op jit(solution)/shard_map/ppermute | solution.py:17
  282.4 29.6 %collective-permute-start.9 = (bf16[2,128,1024]{2,1,0:T(8,128)(2,1)}, bf16[2,128,1024]{2,1,0:T(8,128)(2,1)}, u32[]{:S(2)}, u32[]{:S(2)}) collective-permute-start(bf16[2,128,1024]{2,1,0:T(8,128)(2,1)} %get-tuple-element.483), channel_id=1, source_target_pairs={{2,0},{3,1},{4,2},{5,3},{6,4},{7,5},{8,6},{9,7},{10,8},{11,9},{12,... | collective-permute-start | bytes 1572872 | tf_op jit(solution)/shard_map/ppermute | solution.py:17
  292.4 20.2 %collective-permute-start.8 = (bf16[2,128,1024]{2,1,0:T(8,128)(2,1)}, bf16[2,128,1024]{2,1,0:T(8,128)(2,1)}, u32[]{:S(2)}, u32[]{:S(2)}) collective-permute-start(bf16[2,128,1024]{2,1,0:T(8,128)(2,1)} %get-tuple-element.481), channel_id=1, source_target_pairs={{1,0},{2,1},{3,2},{4,3},{5,4},{6,5},{7,6},{8,7},{9,8},{10,9},{11,1... | collective-permute-start | bytes 1572872 | tf_op jit(solution)/shard_map/ppermute | solution.py:17
Sparse Core Ops, SparseCore 0:
  29.9 76.8 all-gather.1
  141.5 109.0 reduce-scatter.1
  295.0 284.5 all-reduce.1
where the time goes:
time: 590 us; the launch traced here: 588 us
  waiting for transfers between devices  369 us (63%)
  matrix products  85.4 us (14%)
  local copies, waits for them, and re-layouts  56 us (9%)
  starting transfers between devices  49.9 us (8%)
  between operations  14.1 us (2%)
  other arithmetic  12.1 us (2%)
    psum x1, waiting for transfers between devices, body(): weight_sum = lax.psum(row_block, 'seq')  264 us
    ppermute x16, waiting for transfers between devices, shifted(): lax.ppermute(value, axis, [(source, source + steps) for source in range(f...  106 us
    ppermute x16, starting transfers between devices, shifted(): lax.ppermute(value, axis, [(source, source + steps) for source in range(f...  49.6 us
    dot_general x4, matrix products, backward_group(): jnp.einsum('hqk,qhd->khd', grad_score, query_grp, preferred_element_type=...  20.5 us
    sub x8, matrix products, soft_weights(): exponent = jnp.exp(scores - row_peak)  19 us
    dot_general x4, matrix products, backward_group(): jnp.einsum('hqk,khd->qhd', grad_score, key_grp, preferred_element_type=jn...  19 us
  transfers between devices with their start and end apart: 19, of which 12 were waited for; matrix products, arithmetic and copies ran while one was open for 25% of the time, Pallas kernels for 0%

commit v1 on v0

--- a/solution.py
+++ b/solution.py
@@ -105,7 +105,7 @@
         attended, grad_out, (((0,), (0,)), ((), ())), preferred_element_type=jnp.float32
     )
     row_block = lax.psum_scatter(partial_grad, "doc", scatter_dimension=0, tiled=True)
-    weight_sum = lax.psum(row_block, "seq")
+    weight_sum = jnp.sum(lax.all_gather(row_block, "seq"), axis=0)
     grad_weight = weight_sum * (1.0 / math.sqrt(rows_here * seq_count * doc_count))
 
     def backward_group(group_index, grad_state):

time: 590 us -> 522 us (0.88)
  the two profiles are of different devices: /device:TPU:2 before, /device:TPU:94 now
where the time goes in v1:
time: 522 us; the launch traced here: 520 us
  waiting for transfers between devices  265 us (51%)
  starting transfers between devices  87.2 us (17%)
  matrix products  84.7 us (16%)
  local copies, waits for them, and re-layouts  54 us (10%)
  between operations  14.2 us (3%)
  other arithmetic  13.6 us (3%)
    ppermute x16, waiting for transfers between devices, shifted(): lax.ppermute(value, axis, [(source, source + steps) for source in range(f...  127 us
    reduce_scatter x1, waiting for transfers between devices, body(): lax.psum_scatter(partial_grad, 'doc', scatter_dimension=0, tiled=True)  108 us
    ppermute x16, starting transfers between devices, shifted(): lax.ppermute(value, axis, [(source, source + steps) for source in range(f...  86.9 us
    all_gather x1, waiting for transfers between devices, body(): weight_sum = jnp.sum(lax.all_gather(row_block, 'seq'), axis=0)  30.2 us
    dot_general x4, matrix products, backward_group(): jnp.einsum('hqk,qhd->khd', grad_score, query_grp, preferred_element_type=...  20.1 us
    dot_general x4, matrix products, backward_group(): jnp.einsum('hqk,khd->qhd', grad_score, key_grp, preferred_element_type=jn...  19.1 us
    sub x8, matrix products, soft_weights(): exponent = jnp.exp(scores - row_peak)  18.8 us
  transfers between devices with their start and end apart: 19, of which 11 were waited for; matrix products, arithmetic and copies ran while one was open for 28% of the time, Pallas kernels for 0%

profile of v1, /device:TPU:94, one launch (start us, length us, event | category | flops | bytes accessed | tf_op | source)
XLA Modules:
  0.0 519.9 jit_solution(17007499207706110030)
XLA Ops:
  9.6 6.4 %collective-permute-start = (bf16[2,128,1024]{1,2,0:T(8,128)(2,1)S(1)}, bf16[2,128,1024]{1,2,0:T(8,128)(2,1)}, u32[]{:S(2)}, u32[]{:S(2)}) collective-permute-start(bf16[2,128,1024]{1,2,0:T(8,128)(2,1)S(1)} %pad_maximum_fusion.1), channel_id=1, source_target_pairs={{0,4},{1,5},{2,6},{3,7},{4,8},{5,9},{6,10},{7,11},{8,12},{9,13},{1... | collective-permute-start | bytes 1572872 | tf_op jit(solution)/shard_map/ppermute | solution.py:17
  16.0 5.4 %collective-permute-start.1 = (bf16[2,128,1024]{1,2,0:T(8,128)(2,1)S(1)}, bf16[2,128,1024]{1,2,0:T(8,128)(2,1)S(1)}, u32[]{:S(2)}, u32[]{:S(2)}) collective-permute-start(bf16[2,128,1024]{1,2,0:T(8,128)(2,1)S(1)} %pad_maximum_fusion.1), channel_id=1, source_target_pairs={{0,3},{1,4},{2,5},{3,6},{4,7},{5,8},{6,9},{7,10},{8,11},{9,12},{10... | collective-permute-start | bytes 1572872 | tf_op jit(solution)/shard_map/ppermute | solution.py:17
  21.3 3.8 collective-permute-start.2
  25.2 3.2 collective-permute-start.3
  28.4 2.7 collective-permute-start.4
  33.7 16.3 %collective-permute-start.5 = (bf16[2,128,1024]{1,2,0:T(8,128)(2,1)S(1)}, bf16[2,128,1024]{1,2,0:T(8,128)(2,1)S(1)}, u32[]{:S(2)}, u32[]{:S(2)}) collective-permute-start(bf16[2,128,1024]{1,2,0:T(8,128)(2,1)S(1)} %pad_maximum_fusion.1), channel_id=1, source_target_pairs={{2,0},{3,1},{4,2},{5,3},{6,4},{7,5},{8,6},{9,7},{10,8},{11,9},{12,... | collective-permute-start | bytes 1572872 | tf_op jit(solution)/shard_map/ppermute | solution.py:17
  51.2 10.7 %collective-permute-done.1 = bf16[2,128,1024]{1,2,0:T(8,128)(2,1)S(1)} collective-permute-done((bf16[2,128,1024]{1,2,0:T(8,128)(2,1)S(1)}, bf16[2,128,1024]{1,2,0:T(8,128)(2,1)S(1)}, u32[]{:S(2)}, u32[]{:S(2)}) %collective-permute-start.1) | collective-permute-done | bytes 524320 | tf_op jit(solution)/shard_map/ppermute | solution.py:17
  61.9 1.9 collective-permute-start.6
  64.0 9.2 %collective-permute-done.2 = bf16[2,128,1024]{1,2,0:T(8,128)(2,1)S(1)} collective-permute-done((bf16[2,128,1024]{1,2,0:T(8,128)(2,1)S(1)}, bf16[2,128,1024]{1,2,0:T(8,128)(2,1)S(1)}, u32[]{:S(2)}, u32[]{:S(2)}) %collective-permute-start.2) | collective-permute-done | bytes 524320 | tf_op jit(solution)/shard_map/ppermute | solution.py:17
  73.2 1.9 collective-permute-start.7
  75.2 12.7 %collective-permute-done.3 = bf16[2,128,1024]{1,2,0:T(8,128)(2,1)S(1)} collective-permute-done((bf16[2,128,1024]{1,2,0:T(8,128)(2,1)S(1)}, bf16[2,128,1024]{1,2,0:T(8,128)(2,1)S(1)}, u32[]{:S(2)}, u32[]{:S(2)}) %collective-permute-start.3) | collective-permute-done | bytes 524320 | tf_op jit(solution)/shard_map/ppermute | solution.py:17
  88.5 13.9 %collective-permute-done.6 = bf16[2,128,1024]{1,2,0:T(8,128)(2,1)S(1)} collective-permute-done((bf16[2,128,1024]{1,2,0:T(8,128)(2,1)S(1)}, bf16[2,128,1024]{1,2,0:T(8,128)(2,1)S(1)}, u32[]{:S(2)}, u32[]{:S(2)}) %collective-permute-start.6) | collective-permute-done | bytes 524320 | tf_op jit(solution)/shard_map/ppermute | solution.py:17
  102.6 2.6 slice_bitcast_fusion
  105.2 29.0 %while.38 = (s32[]{:T(128)}, bf16[128,1024]{0,1:T(8,128)(2,1)S(1)}, bf16[1152,1024]{0,1:T(8,128)(2,1)}, bf16[128,1024]{0,1:T(8,128)(2,1)}, bf16[1152,1024]{0,1:T...) while((s32[]{:T(128)}, bf16[128,1024]{0,1:T(8,128)(2,1)S(1)}, ...), condition=%wide.region_6.7_spmd.clone, body=%wide.region_3.6_spmd.clone.sunk | while | flops 155452544 | bytes 8961351 | solution.py:93
  105.3 1.4 constant_dynamic-slice_fusion.13
  107.8 2.4 fusion.104
  110.2 2.3 fusion.105
  112.5 1.3 constant_dynamic-slice_fusion.13
  115.0 2.4 fusion.104
  117.4 2.3 fusion.105
  119.8 1.3 constant_dynamic-slice_fusion.13
  122.3 2.4 fusion.104
  124.6 2.3 fusion.105
  127.0 1.3 constant_dynamic-slice_fusion.13
  129.5 2.4 fusion.104
  131.9 2.3 fusion.105
  134.2 2.7 fusion.51
  137.2 3.1 convolution_convert_fusion
  140.4 107.6 %reduce-scatter.2.cloned.1.call-done = f32[64,1024]{1,0:T(8,128)} async-done(((f32[1024,1024]{1,0:T(8,128)}), f32[64,1024]{1,0:T(8,128)}) %reduce-scatter.2.cloned.1.call-update) | async-done | bytes 262160 | tf_op jit(solution)/shard_map/reduce_scatter | solution.py:107
  249.9 1.6 broadcast.133.clone
  251.5 1.6 broadcast.133.clone2
  253.1 93.9 %while.39 = (s32[]{:T(128)}, bf16[128,1024]{1,0:T(8,128)(2,1)}, f32[2,128,1024]{2,1,0:T(8,128)}, bf16[2,512,1024]{2,1,0:T(8,128)(2,1)}, bf16[2,512,1024]{2,1,0:T...) while((s32[]{:T(128)}, bf16[128,1024]{1,0:T(8,128)(2,1)}, ...), condition=%wide.region_12.13_spmd.clone, body=%wide.region_8.12_spmd.clone.sunk | while | flops 390861184 | bytes 38351472 | solution.py:157
  258.7 2.3 fusion.118
  261.0 4.7 fusion.119
  266.6 5.1 fusion.120
  271.7 2.1 fusion.121
  282.2 2.3 fusion.118
  284.6 4.8 fusion.119
  290.1 5.0 fusion.120
  295.1 2.1 fusion.121
  305.7 2.3 fusion.118
  308.1 4.8 fusion.119
  313.6 5.0 fusion.120
  318.6 2.1 fusion.121
  329.2 2.3 fusion.118
  331.5 4.8 fusion.119
  337.0 5.0 fusion.120
  342.1 2.1 fusion.121
  347.0 1.8 fusion.58
  348.9 5.8 %collective-permute-start.15 = (bf16[2,128,1024]{2,1,0:T(8,128)(2,1)S(1)}, bf16[2,128,1024]{2,1,0:T(8,128)(2,1)S(1)}, u32[]{:S(2)}, u32[]{:S(2)}) collective-permute-start(bf16[2,128,1024]{2,1,0:T(8,128)(2,1)S(1)} %get-tuple-element.488), channel_id=1, source_target_pairs={{0,4},{1,5},{2,6},{3,7},{4,8},{5,9},{6,10},{7,11},{8,12},{9,13},{1... | collective-permute-start | bytes 1572872 | tf_op jit(solution)/shard_map/ppermute | solution.py:17
  354.7 3.6 collective-permute-start.14
  358.3 3.4 collective-permute-start.13
  361.7 4.3 collective-permute-start.12
  366.2 2.5 collective-permute-start.11
  368.7 8.6 %collective-permute-done.15 = bf16[2,128,1024]{2,1,0:T(8,128)(2,1)S(1)} collective-permute-done((bf16[2,128,1024]{2,1,0:T(8,128)(2,1)S(1)}, bf16[2,128,1024]{2,1,0:T(8,128)(2,1)S(1)}, u32[]{:S(2)}, u32[]{:S(2)}) %collective-permute-start.15) | collective-permute-done | bytes 524320 | tf_op jit(solution)/shard_map/ppermute | solution.py:17
  377.3 1.9 collective-permute-start.10
  379.2 16.6 %collective-permute-done.14 = bf16[2,128,1024]{2,1,0:T(8,128)(2,1)S(1)} collective-permute-done((bf16[2,128,1024]{2,1,0:T(8,128)(2,1)S(1)}, bf16[2,128,1024]{2,1,0:T(8,128)(2,1)S(1)}, u32[]{:S(2)}, u32[]{:S(2)}) %collective-permute-start.14) | collective-permute-done | bytes 524320 | tf_op jit(solution)/shard_map/ppermute | solution.py:17
  395.8 22.0 %collective-permute-start.9 = (bf16[2,128,1024]{2,1,0:T(8,128)(2,1)S(1)}, bf16[2,128,1024]{2,1,0:T(8,128)(2,1)S(1)}, u32[]{:S(2)}, u32[]{:S(2)}) collective-permute-start(bf16[2,128,1024]{2,1,0:T(8,128)(2,1)S(1)} %get-tuple-element.483), channel_id=1, source_target_pairs={{2,0},{3,1},{4,2},{5,3},{6,4},{7,5},{8,6},{9,7},{10,8},{11,9},{12,... | collective-permute-start | bytes 1572872 | tf_op jit(solution)/shard_map/ppermute | solution.py:17
  417.8 18.2 %collective-permute-done.13 = bf16[2,128,1024]{2,1,0:T(8,128)(2,1)S(1)} collective-permute-done((bf16[2,128,1024]{2,1,0:T(8,128)(2,1)S(1)}, bf16[2,128,1024]{2,1,0:T(8,128)(2,1)S(1)}, u32[]{:S(2)}, u32[]{:S(2)}) %collective-permute-start.13) | collective-permute-done | bytes 524320 | tf_op jit(solution)/shard_map/ppermute | solution.py:17
  436.1 1.9 collective-permute-start.8
  439.2 10.7 %collective-permute-done.12 = bf16[2,128,1024]{2,1,0:T(8,128)(2,1)S(1)} collective-permute-done((bf16[2,128,1024]{2,1,0:T(8,128)(2,1)S(1)}, bf16[2,128,1024]{2,1,0:T(8,128)(2,1)S(1)}, u32[]{:S(2)}, u32[]{:S(2)}) %collective-permute-start.12) | collective-permute-done | bytes 524320 | tf_op jit(solution)/shard_map/ppermute | solution.py:17
  449.9 26.8 %collective-permute-done.8 = bf16[2,128,1024]{2,1,0:T(8,128)(2,1)S(1)} collective-permute-done((bf16[2,128,1024]{2,1,0:T(8,128)(2,1)S(1)}, bf16[2,128,1024]{2,1,0:T(8,128)(2,1)S(1)}, u32[]{:S(2)}, u32[]{:S(2)}) %collective-permute-start.8) | collective-permute-done | bytes 524320 | tf_op jit(solution)/shard_map/ppermute | solution.py:17
  478.5 30.2 %all-gather.6.cloned.1.call-done = f32[2048,1024]{1,0:T(8,128)} async-done(((f32[64,1024]{1,0:T(8,128)}), f32[2048,1024]{1,0:T(8,128)}) %all-gather.6.cloned.1.call-update) | async-done | bytes 8388624 | tf_op jit(solution)/shard_map/all_gather | solution.py:108
  508.7 4.0 reduce_sum.78
  (210 shorter events, 54.2 us)
Async XLA Ops:
  7.2 25.6 %copy-start.8 = (bf16[1,128,1024]{2,1,0:T(8,128)(2,1)S(1)}, bf16[1,128,1024]{2,1,0:T(8,128)(2,1)}, u32[]{:S(2)}) copy-start(bf16[1,128,1024]{2,1,0:T(8,128)(2,1)} %param.19) | copy-start | bytes 786436
  7.2 130.1 %all-gather.4.cloned.1.call-start = ((), (), s32[]{:S(2)}) async-start(), calls=%async_computation.1 | async-start | bytes 2228224 | tf_op jit(solution)/shard_map/all_gather | solution.py:96
  9.6 24.2 %collective-permute-start = (bf16[2,128,1024]{1,2,0:T(8,128)(2,1)S(1)}, bf16[2,128,1024]{1,2,0:T(8,128)(2,1)}, u32[]{:S(2)}, u32[]{:S(2)}) collective-permute-start(bf16[2,128,1024]{1,2,0:T(8,128)(2,1)S(1)} %pad_maximum_fusion.1), channel_id=1, source_target_pairs={{0,4},{1,5},{2,6},{3,7},{4,8},{5,9},{6,10},{7,11},{8,12},{9,13},{1... | collective-permute-start | bytes 1572872 | tf_op jit(solution)/shard_map/ppermute | solution.py:17
  16.0 46.0 %collective-permute-start.1 = (bf16[2,128,1024]{1,2,0:T(8,128)(2,1)S(1)}, bf16[2,128,1024]{1,2,0:T(8,128)(2,1)S(1)}, u32[]{:S(2)}, u32[]{:S(2)}) collective-permute-start(bf16[2,128,1024]{1,2,0:T(8,128)(2,1)S(1)} %pad_maximum_fusion.1), channel_id=1, source_target_pairs={{0,3},{1,4},{2,5},{3,6},{4,7},{5,8},{6,9},{7,10},{8,11},{9,12},{10... | collective-permute-start | bytes 1572872 | tf_op jit(solution)/shard_map/ppermute | solution.py:17
  21.3 51.8 %collective-permute-start.2 = (bf16[2,128,1024]{1,2,0:T(8,128)(2,1)S(1)}, bf16[2,128,1024]{1,2,0:T(8,128)(2,1)S(1)}, u32[]{:S(2)}, u32[]{:S(2)}) collective-permute-start(bf16[2,128,1024]{1,2,0:T(8,128)(2,1)S(1)} %pad_maximum_fusion.1), channel_id=1, source_target_pairs={{0,2},{1,3},{2,4},{3,5},{4,6},{5,7},{6,8},{7,9},{8,10},{9,11},{10,... | collective-permute-start | bytes 1572872 | tf_op jit(solution)/shard_map/ppermute | solution.py:17
  25.2 62.7 %collective-permute-start.3 = (bf16[2,128,1024]{1,2,0:T(8,128)(2,1)S(1)}, bf16[2,128,1024]{1,2,0:T(8,128)(2,1)S(1)}, u32[]{:S(2)}, u32[]{:S(2)}) collective-permute-start(bf16[2,128,1024]{1,2,0:T(8,128)(2,1)S(1)} %pad_maximum_fusion.1), channel_id=1, source_target_pairs={{0,1},{1,2},{2,3},{3,4},{4,5},{5,6},{6,7},{7,8},{8,9},{9,10},{10,1... | collective-permute-start | bytes 1572872 | tf_op jit(solution)/shard_map/ppermute | solution.py:17
  28.4 59.8 %collective-permute-start.4 = (bf16[2,128,1024]{1,2,0:T(8,128)(2,1)S(1)}, bf16[2,128,1024]{1,2,0:T(8,128)(2,1)S(1)}, u32[]{:S(2)}, u32[]{:S(2)}) collective-permute-start(bf16[2,128,1024]{1,2,0:T(8,128)(2,1)S(1)} %pad_maximum_fusion.1), channel_id=1, source_target_pairs={{1,0},{2,1},{3,2},{4,3},{5,4},{6,5},{7,6},{8,7},{9,8},{10,9},{11,1... | collective-permute-start | bytes 1572872 | tf_op jit(solution)/shard_map/ppermute | solution.py:17
  31.0 216.9 %reduce-scatter.2.cloned.1.call-start = ((), (), s32[]{:S(2)}) async-start(), calls=%async_computation.2 | async-start | bytes 4456448 | tf_op jit(solution)/shard_map/reduce_scatter | solution.py:107
  33.7 54.6 %collective-permute-start.5 = (bf16[2,128,1024]{1,2,0:T(8,128)(2,1)S(1)}, bf16[2,128,1024]{1,2,0:T(8,128)(2,1)S(1)}, u32[]{:S(2)}, u32[]{:S(2)}) collective-permute-start(bf16[2,128,1024]{1,2,0:T(8,128)(2,1)S(1)} %pad_maximum_fusion.1), channel_id=1, source_target_pairs={{2,0},{3,1},{4,2},{5,3},{6,4},{7,5},{8,6},{9,7},{10,8},{11,9},{12,... | collective-permute-start | bytes 1572872 | tf_op jit(solution)/shard_map/ppermute | solution.py:17
  61.9 40.4 %collective-permute-start.6 = (bf16[2,128,1024]{1,2,0:T(8,128)(2,1)S(1)}, bf16[2,128,1024]{1,2,0:T(8,128)(2,1)S(1)}, u32[]{:S(2)}, u32[]{:S(2)}) collective-permute-start(bf16[2,128,1024]{1,2,0:T(8,128)(2,1)S(1)} %pad_maximum_fusion.1), channel_id=1, source_target_pairs={{3,0},{4,1},{5,2},{6,3},{7,4},{8,5},{9,6},{10,7},{11,8},{12,9},{13... | collective-permute-start | bytes 1572872 | tf_op jit(solution)/shard_map/ppermute | solution.py:17
  73.2 29.3 %collective-permute-start.7 = (bf16[2,128,1024]{1,2,0:T(8,128)(2,1)S(1)}, bf16[2,128,1024]{1,2,0:T(8,128)(2,1)S(1)}, u32[]{:S(2)}, u32[]{:S(2)}) collective-permute-start(bf16[2,128,1024]{1,2,0:T(8,128)(2,1)S(1)} %pad_maximum_fusion.1), channel_id=1, source_target_pairs={{4,0},{5,1},{6,2},{7,3},{8,4},{9,5},{10,6},{11,7},{12,8},{13,9},{1... | collective-permute-start | bytes 1572872 | tf_op jit(solution)/shard_map/ppermute | solution.py:17
  105.2 29.0 %copy-start.7 = (bf16[1,128,1024]{2,1,0:T(8,128)(2,1)S(1)}, bf16[1,128,1024]{2,1,0:T(8,128)(2,1)}, u32[]{:S(2)}) copy-start(bf16[1,128,1024]{2,1,0:T(8,128)(2,1)} %param.22) | copy-start | bytes 786436
  134.2 2.8 copy-start.4
  137.0 371.7 %all-gather.6.cloned.1.call-start = ((), (), s32[]{:S(2)}) async-start(), calls=%async_computation.3 | async-start | bytes 8650752 | tf_op jit(solution)/shard_map/all_gather | solution.py:108
  253.1 3.2 copy-start.9
  253.1 3.3 copy-start.11
  253.1 3.3 copy-start.13
  255.2 5.8 %copy-start.2 = (bf16[128,256]{0,1:T(8,128)(2,1)}, bf16[128,256]{0,1:T(8,128)(2,1)S(1)}, u32[]{:S(2)}) copy-start(bf16[128,256]{0,1:T(8,128)(2,1)S(1)} %copy.55) | copy-start | bytes 196612 | tf_op jit(solution)/shard_map/while
  257.7 8.0 %copy-start.6 = (bf16[128,256]{0,1:T(8,128)(2,1)}, bf16[128,256]{0,1:T(8,128)(2,1)S(1)}, u32[]{:S(2)}) copy-start(bf16[128,256]{0,1:T(8,128)(2,1)S(1)} %constant_dynamic-slice_fusion.18) | copy-start | bytes 196612 | tf_op jit(solution)/shard_map/while
  261.0 4.8 copy-start.15
  275.0 1.6 copy-start.10
  275.0 1.6 copy-start.12
  275.0 1.6 copy-start.14
  276.6 3.3 copy-start.9
  276.6 3.3 copy-start.11
  276.6 3.3 copy-start.13
  278.7 5.9 %copy-start.2 = (bf16[128,256]{0,1:T(8,128)(2,1)}, bf16[128,256]{0,1:T(8,128)(2,1)S(1)}, u32[]{:S(2)}) copy-start(bf16[128,256]{0,1:T(8,128)(2,1)S(1)} %copy.55) | copy-start | bytes 196612 | tf_op jit(solution)/shard_map/while
  281.3 8.1 %copy-start.6 = (bf16[128,256]{0,1:T(8,128)(2,1)}, bf16[128,256]{0,1:T(8,128)(2,1)S(1)}, u32[]{:S(2)}) copy-start(bf16[128,256]{0,1:T(8,128)(2,1)S(1)} %constant_dynamic-slice_fusion.18) | copy-start | bytes 196612 | tf_op jit(solution)/shard_map/while
  284.6 4.8 copy-start.15
  298.5 1.6 copy-start.10
  298.5 1.5 copy-start.12
  298.5 1.5 copy-start.14
  300.1 3.3 copy-start.9
  300.1 3.3 copy-start.11
  300.1 3.3 copy-start.13
  302.2 5.8 %copy-start.2 = (bf16[128,256]{0,1:T(8,128)(2,1)}, bf16[128,256]{0,1:T(8,128)(2,1)S(1)}, u32[]{:S(2)}) copy-start(bf16[128,256]{0,1:T(8,128)(2,1)S(1)} %copy.55) | copy-start | bytes 196612 | tf_op jit(solution)/shard_map/while
  304.8 8.1 %copy-start.6 = (bf16[128,256]{0,1:T(8,128)(2,1)}, bf16[128,256]{0,1:T(8,128)(2,1)S(1)}, u32[]{:S(2)}) copy-start(bf16[128,256]{0,1:T(8,128)(2,1)S(1)} %constant_dynamic-slice_fusion.18) | copy-start | bytes 196612 | tf_op jit(solution)/shard_map/while
  308.1 4.8 copy-start.15
  321.9 1.5 copy-start.10
  322.0 1.5 copy-start.12
  322.0 1.5 copy-start.14
  323.5 3.3 copy-start.9
  323.5 3.3 copy-start.11
  323.5 3.3 copy-start.13
  325.6 5.9 %copy-start.2 = (bf16[128,256]{0,1:T(8,128)(2,1)}, bf16[128,256]{0,1:T(8,128)(2,1)S(1)}, u32[]{:S(2)}) copy-start(bf16[128,256]{0,1:T(8,128)(2,1)S(1)} %copy.55) | copy-start | bytes 196612 | tf_op jit(solution)/shard_map/while
  328.2 8.1 %copy-start.6 = (bf16[128,256]{0,1:T(8,128)(2,1)}, bf16[128,256]{0,1:T(8,128)(2,1)S(1)}, u32[]{:S(2)}) copy-start(bf16[128,256]{0,1:T(8,128)(2,1)S(1)} %constant_dynamic-slice_fusion.18) | copy-start | bytes 196612 | tf_op jit(solution)/shard_map/while
  331.5 4.8 copy-start.15
  345.4 1.6 copy-start.10
  345.4 1.6 copy-start.12
  345.4 1.6 copy-start.14
  347.0 19.0 %copy-start.1 = (bf16[2,512,1024]{2,1,0:T(8,128)(2,1)S(1)}, bf16[2,512,1024]{2,1,0:T(8,128)(2,1)}, u32[]{:S(2)}) copy-start(bf16[2,512,1024]{2,1,0:T(8,128)(2,1)} %get-tuple-element.329) | copy-start | bytes 6291460
  348.9 89.1 %copy-start = (bf16[1024,1024]{1,0:T(8,128)(2,1)S(1)}, bf16[1024,1024]{1,0:T(8,128)(2,1)}, u32[]{:S(2)}) copy-start(bf16[1024,1024]{1,0:T(8,128)(2,1)} %all-gather.4.cloned.1.call-done) | copy-start | bytes 6291460
  348.9 89.1 %copy-start.5 = (bf16[128,1024]{0,1:T(8,128)(2,1)S(1)}, bf16[128,1024]{0,1:T(8,128)(2,1)}, u32[]{:S(2)}) copy-start(bf16[128,1024]{0,1:T(8,128)(2,1)} %copy-done.4) | copy-start | bytes 786436
  348.9 28.4 %collective-permute-start.15 = (bf16[2,128,1024]{2,1,0:T(8,128)(2,1)S(1)}, bf16[2,128,1024]{2,1,0:T(8,128)(2,1)S(1)}, u32[]{:S(2)}, u32[]{:S(2)}) collective-permute-start(bf16[2,128,1024]{2,1,0:T(8,128)(2,1)S(1)} %get-tuple-element.488), channel_id=1, source_target_pairs={{0,4},{1,5},{2,6},{3,7},{4,8},{5,9},{6,10},{7,11},{8,12},{9,13},{1... | collective-permute-start | bytes 1572872 | tf_op jit(solution)/shard_map/ppermute | solution.py:17
  354.7 41.1 %collective-permute-start.14 = (bf16[2,128,1024]{2,1,0:T(8,128)(2,1)S(1)}, bf16[2,128,1024]{2,1,0:T(8,128)(2,1)S(1)}, u32[]{:S(2)}, u32[]{:S(2)}) collective-permute-start(bf16[2,128,1024]{2,1,0:T(8,128)(2,1)S(1)} %get-tuple-element.486), channel_id=1, source_target_pairs={{0,3},{1,4},{2,5},{3,6},{4,7},{5,8},{6,9},{7,10},{8,11},{9,12},{10... | collective-permute-start | bytes 1572872 | tf_op jit(solution)/shard_map/ppermute | solution.py:17
  358.3 77.8 %collective-permute-start.13 = (bf16[2,128,1024]{2,1,0:T(8,128)(2,1)S(1)}, bf16[2,128,1024]{2,1,0:T(8,128)(2,1)S(1)}, u32[]{:S(2)}, u32[]{:S(2)}) collective-permute-start(bf16[2,128,1024]{2,1,0:T(8,128)(2,1)S(1)} %get-tuple-element.487), channel_id=1, source_target_pairs={{0,2},{1,3},{2,4},{3,5},{4,6},{5,7},{6,8},{7,9},{8,10},{9,11},{10,... | collective-permute-start | bytes 1572872 | tf_op jit(solution)/shard_map/ppermute | solution.py:17
  361.7 88.2 %collective-permute-start.12 = (bf16[2,128,1024]{2,1,0:T(8,128)(2,1)S(1)}, bf16[2,128,1024]{2,1,0:T(8,128)(2,1)S(1)}, u32[]{:S(2)}, u32[]{:S(2)}) collective-permute-start(bf16[2,128,1024]{2,1,0:T(8,128)(2,1)S(1)} %get-tuple-element.485), channel_id=1, source_target_pairs={{0,1},{1,2},{2,3},{3,4},{4,5},{5,6},{6,7},{7,8},{8,9},{9,10},{10,1... | collective-permute-start | bytes 1572872 | tf_op jit(solution)/shard_map/ppermute | solution.py:17
  366.2 110.5 %copy-start.3 = (f32[2,128,1024]{2,1,0:T(8,128)S(1)}, f32[2,128,1024]{2,1,0:T(8,128)}, u32[]{:S(2)}) copy-start(f32[2,128,1024]{2,1,0:T(8,128)} %get-tuple-element.328) | copy-start | bytes 3145732
  366.2 83.7 %collective-permute-start.11 = (bf16[2,128,1024]{2,1,0:T(8,128)(2,1)S(1)}, bf16[2,128,1024]{2,1,0:T(8,128)(2,1)S(1)}, u32[]{:S(2)}, u32[]{:S(2)}) collective-permute-start(bf16[2,128,1024]{2,1,0:T(8,128)(2,1)S(1)} %get-tuple-element.484), channel_id=1, source_target_pairs={{4,0},{5,1},{6,2},{7,3},{8,4},{9,5},{10,6},{11,7},{12,8},{13,9},{1... | collective-permute-start | bytes 1572872 | tf_op jit(solution)/shard_map/ppermute | solution.py:17
  377.3 72.6 %collective-permute-start.10 = (bf16[2,128,1024]{2,1,0:T(8,128)(2,1)S(1)}, bf16[2,128,1024]{2,1,0:T(8,128)(2,1)S(1)}, u32[]{:S(2)}, u32[]{:S(2)}) collective-permute-start(bf16[2,128,1024]{2,1,0:T(8,128)(2,1)S(1)} %get-tuple-element.482), channel_id=1, source_target_pairs={{3,0},{4,1},{5,2},{6,3},{7,4},{8,5},{9,6},{10,7},{11,8},{12,9},{13... | collective-permute-start | bytes 1572872 | tf_op jit(solution)/shard_map/ppermute | solution.py:17
  395.8 54.1 %collective-permute-start.9 = (bf16[2,128,1024]{2,1,0:T(8,128)(2,1)S(1)}, bf16[2,128,1024]{2,1,0:T(8,128)(2,1)S(1)}, u32[]{:S(2)}, u32[]{:S(2)}) collective-permute-start(bf16[2,128,1024]{2,1,0:T(8,128)(2,1)S(1)} %get-tuple-element.483), channel_id=1, source_target_pairs={{2,0},{3,1},{4,2},{5,3},{6,4},{7,5},{8,6},{9,7},{10,8},{11,9},{12,... | collective-permute-start | bytes 1572872 | tf_op jit(solution)/shard_map/ppermute | solution.py:17
  436.1 40.7 %collective-permute-start.8 = (bf16[2,128,1024]{2,1,0:T(8,128)(2,1)S(1)}, bf16[2,128,1024]{2,1,0:T(8,128)(2,1)S(1)}, u32[]{:S(2)}, u32[]{:S(2)}) collective-permute-start(bf16[2,128,1024]{2,1,0:T(8,128)(2,1)S(1)} %get-tuple-element.481), channel_id=1, source_target_pairs={{1,0},{2,1},{3,2},{4,3},{5,4},{6,5},{7,6},{8,7},{9,8},{10,9},{11,1... | collective-permute-start | bytes 1572872 | tf_op jit(solution)/shard_map/ppermute | solution.py:17
Sparse Core Ops, SparseCore 0:
  31.2 70.5 all-gather.3
  137.1 110.8 reduce-scatter.1
  250.3 258.3 all-gather.5
